TPU v7x, 32 devices: a whole 2x2x4 slice. The times are simulated.
32 devices in a mesh: az: 16 (over z, y, x), rad: 2 (over core).
Axes of the slice: x: 2, y: 2, z: 4, core: 2. Of those that a mesh axis runs over, the one named last changes fastest.
Arguments:
- state: float32 [5, 2, 512, 256], P(None, None, 'az', 'rad'), as said below
- shifts: int32 [256], P('rad'), may hold values from 4 to 96, as said below
Outputs:
- state_out: float32 [5, 2, 512, 256], P(None, None, 'az', 'rad')
Inputs may be any that keep to these rules, and one draw needn't show every extreme that they name: `state`: density lies between 0.3 and 3, each velocity component (momentum over density) between -1 and 1, and energy exceeds the kinetic energy by at least 0.8 times density. `shifts`: both 4 and 96 occur.
All inputs are finite; a program needn't handle non-finite values.
Results may differ from a plain program's by a relative error of at most 0.0003.
Values sent between devices are 32-bit elements; how exact they have to be, the bound alone decides.
A program may use at most 64 MiB of HBM per device.

v0:
```python
import jax
import jax.numpy as jnp
from jax import lax
from jax.sharding import PartitionSpec as P

STEPS = 2
SMAX = 96


GAMMA_GAS = 1.4
COURANT_RADIAL = 0.15
COURANT_AZIMUTH = 0.15
VISCOSITY_COEF = 1.0


def padded(block, sides, width, periodic):
    for axis, dim in sides:
        count = lax.axis_size(axis)
        forward = [(i, i + 1) for i in range(count - 1)]
        if periodic:
            forward.append((count - 1, 0))
        backward = [(target, source) for source, target in forward]
        low = lax.ppermute(
            lax.slice_in_dim(block, block.shape[dim] - width, None, axis=dim), axis, forward
        )
        high = lax.ppermute(lax.slice_in_dim(block, 0, width, axis=dim), axis, backward)
        block = jnp.concatenate([low, block, high], axis=dim)
    return block


def from_behind(x, axis, by):
    peers = lax.axis_size(axis)
    return lax.ppermute(x, axis, [(i, (i + by) % peers) for i in range(peers)])


def cut(array, start, stop, axis):
    return lax.slice_in_dim(array, start, stop, axis=axis)


def van_leer(left_diff, right_diff):
    product = left_diff * right_diff
    positive = product > 0
    safe_sum = jnp.where(positive, left_diff + right_diff, 1.0)
    return jnp.where(positive, 2.0 * product / safe_sum, 0.0)


def transport(strip, axis, component, courant):
    length = strip.shape[axis] - 4
    velocity = strip[component : component + 1] / strip[0:1]
    diffs = cut(strip, 1, length + 4, axis) - cut(strip, 0, length + 3, axis)
    slopes = van_leer(cut(diffs, 0, length + 2, axis), cut(diffs, 1, length + 3, axis))
    left_state = cut(strip, 1, length + 2, axis) + 0.5 * cut(slopes, 0, length + 1, axis)
    right_state = cut(strip, 2, length + 3, axis) - 0.5 * cut(slopes, 1, length + 2, axis)
    face_speed = 0.5 * (cut(velocity, 1, length + 2, axis) + cut(velocity, 2, length + 3, axis))
    flux = jnp.maximum(face_speed, 0.0) * left_state + jnp.minimum(face_speed, 0.0) * right_state
    return -courant * (cut(flux, 1, length + 1, axis) - cut(flux, 0, length, axis))


def pressure_push(strip, axis, component, courant):
    length = strip.shape[axis] - 4
    density = strip[0:1]
    momenta = strip[1:4]
    speed = strip[component : component + 1] / density
    pressure = (GAMMA_GAS - 1.0) * (
        strip[4:5] - 0.5 * jnp.sum(momenta * momenta, axis=0, keepdims=True) / density
    )
    compress = jnp.minimum(cut(speed, 2, length + 4, axis) - cut(speed, 0, length + 2, axis), 0.0)
    total = (
        cut(pressure, 1, length + 3, axis)
        + VISCOSITY_COEF * cut(density, 1, length + 3, axis) * compress * compress
    )
    work = total * cut(speed, 1, length + 3, axis)
    gradient = 0.5 * (cut(total, 2, length + 2, axis) - cut(total, 0, length, axis))
    work_div = 0.5 * (cut(work, 2, length + 2, axis) - cut(work, 0, length, axis))
    zeros = jnp.zeros_like(gradient)
    pieces = [zeros, zeros, zeros, zeros, -courant * work_div]
    pieces[component] = -courant * gradient
    return jnp.concatenate(pieces, axis=0)


def hydro(state, az_strip, rad_strip):
    return (
        state
        + transport(az_strip, 2, 2, COURANT_AZIMUTH)
        + transport(rad_strip, 3, 1, COURANT_RADIAL)
    )


def viscous(state, az_strip, rad_strip):
    return (
        state
        + pressure_push(az_strip, 2, 2, COURANT_AZIMUTH)
        + pressure_push(rad_strip, 3, 1, COURANT_RADIAL)
    )


def strips(state):
    az_strip = padded(state, (("az", 2),), 2, True)
    rad_strip = padded(state, (("rad", 3),), 2, False)
    position = lax.axis_index("rad")
    count = lax.axis_size("rad")
    lower = jnp.where(
        position == 0, jnp.repeat(rad_strip[:, :, :, 2:3], 2, axis=3), rad_strip[:, :, :, :2]
    )
    upper = jnp.where(
        position == count - 1,
        jnp.repeat(rad_strip[:, :, :, -3:-2], 2, axis=3),
        rad_strip[:, :, :, -2:],
    )
    rad_strip = jnp.concatenate([lower, rad_strip[:, :, :, 2:-2], upper], axis=3)
    return (az_strip, rad_strip)


def barrel_roll(paired, remainder, width):
    nbits = (width - 1).bit_length()
    padding = (1 << nbits) - width
    rolled = paired
    for bit in range(nbits):
        stride = 1 << bit
        length = rolled.shape[2] - stride
        taken = (remainder >> bit & 1 == 1)[None, None, None, :]
        rolled = jnp.where(
            taken, cut(rolled, 0, length, 2), cut(rolled, stride, stride + length, 2)
        )
    return cut(rolled, 1, width + 1, 2)


def rotate(state, shifts):
    width = state.shape[2]
    whole_hops = shifts // width
    remainder = shifts % width
    paired = jnp.concatenate([from_behind(state, "az", 1), state], axis=2)
    for bit in range((SMAX // width).bit_length()):
        moved = from_behind(paired, "az", 1 << bit)
        paired = jnp.where((whole_hops >> bit & 1 == 1)[None, None, None, :], moved, paired)
    return barrel_roll(paired, remainder, width)


def body(state, shifts):
    for step in range(STEPS):
        az_strip, rad_strip = strips(state)
        state = hydro(state, az_strip, rad_strip)
        state = rotate(state, shifts)
        az_strip, rad_strip = strips(state)
        state = viscous(state, az_strip, rad_strip)
    return state


def solution(mesh):
    in_specs = (P(None, None, "az", "rad"), P("rad"))
    out_specs = P(None, None, "az", "rad")
    return jax.shard_map(body, mesh=mesh, in_specs=in_specs, out_specs=out_specs, check_vma=False)
```

profile of v0, /device:TPU:1, one launch (start us, length us, event | category | flops | bytes accessed | tf_op | source)
XLA Modules:
  0.0 121.2 jit_solution(471273838386067631)
XLA Ops:
  0.0 1.2 fusion.79
  1.2 1.9 %collective-permute-start.3 = (f32[5,2,32,2]{3,2,1,0:T(8,128)S(1)}, f32[5,2,32,2]{3,2,1,0:T(8,128)S(1)}, u32[]{:S(2)}, u32[]{:S(2)}) collective-permute-start(f32[5,2,32,2]{3,2,1,0:T(8,128)S(1)} %get-tuple-element.52), channel_id=1, source_target_pairs={{1,0},{3,2},{5,4},{7,6},{9,8},{11,10},{13,12},{15,14},{17,16},{19,... | collective-permute-start | bytes 7688 | tf_op jit(solution)/shard_map/ppermute | solution.py:26
  3.1 1.3 %collective-permute-start.2 = (f32[5,2,32,2]{3,2,1,0:T(8,128)S(1)}, f32[5,2,32,2]{3,2,1,0:T(8,128)S(1)}, u32[]{:S(2)}, u32[]{:S(2)}) collective-permute-start(f32[5,2,32,2]{3,2,1,0:T(8,128)S(1)} %get-tuple-element.51), channel_id=1, source_target_pairs={{0,1},{2,3},{4,5},{6,7},{8,9},{10,11},{12,13},{14,15},{16,17},{18,... | collective-permute-start | bytes 7688 | tf_op jit(solution)/shard_map/ppermute | solution.py:23
  4.4 6.7 %collective-permute-start.1 = (f32[5,2,2,128]{3,2,1,0:T(2,128)S(1)}, f32[5,2,2,128]{3,2,1,0:T(2,128)S(1)}, u32[]{:S(2)}, u32[]{:S(2)}) collective-permute-start(f32[5,2,2,128]{3,2,1,0:T(2,128)S(1)} %get-tuple-element.50), channel_id=1, source_target_pairs={{2,0},{4,2},{6,4},{8,6},{10,8},{12,10},{14,12},{16,14},{18,16},{20... | collective-permute-start | bytes 30728 | tf_op jit(solution)/shard_map/ppermute | solution.py:26
  11.2 0.2 slice_reduce_fusion.7
  11.7 0.2 pad_maximum_fusion.4
  11.9 0.1 maximum_divide_fusion.1
  12.0 0.1 slice_subtract_fusion.1
  12.1 0.2 divide_select_fusion.1
  12.4 0.3 fusion.7
  12.7 4.6 %collective-permute-done = f32[5,2,2,128]{3,2,1,0:T(2,128)S(1)} collective-permute-done((f32[5,2,2,128]{3,2,1,0:T(2,128)S(1)}, f32[5,2,2,128]{3,2,1,0:T(2,128)S(1)}, u32[]{:S(2)}, u32[]{:S(2)}) %collective-permute-start) | collective-permute-done | bytes 10272 | tf_op jit(solution)/shard_map/ppermute | solution.py:23
  17.6 0.1 fusion.35
  17.8 7.8 %collective-permute-done.4 = f32[5,2,32,128]{3,2,1,0:T(8,128)S(1)} collective-permute-done((f32[5,2,32,128]{3,2,1,0:T(8,128)S(1)}, f32[5,2,32,128]{3,2,1,0:T(8,128)S(1)}, u32[]{:S(2)}, u32[]{:S(2)}) %collective-permute-start.4) | collective-permute-done | bytes 163872 | tf_op jit(solution)/shard_map/ppermute | solution.py:33
  25.7 9.5 %collective-permute-done.5 = f32[5,2,64,128]{3,2,1,0:T(8,128)S(1)} collective-permute-done((f32[5,2,64,128]{3,2,1,0:T(8,128)S(1)}, f32[5,2,64,128]{3,2,1,0:T(8,128)S(1)}, u32[]{:S(2)}, u32[]{:S(2)}) %collective-permute-start.5) | collective-permute-done | bytes 327712 | tf_op jit(solution)/shard_map/ppermute | solution.py:33
  35.3 9.5 %collective-permute-done.6 = f32[5,2,64,128]{3,2,1,0:T(8,128)S(1)} collective-permute-done((f32[5,2,64,128]{3,2,1,0:T(8,128)S(1)}, f32[5,2,64,128]{3,2,1,0:T(8,128)S(1)}, u32[]{:S(2)}, u32[]{:S(2)}) %collective-permute-start.6) | collective-permute-done | bytes 327712 | tf_op jit(solution)/shard_map/ppermute | solution.py:33
  45.0 0.1 fusion.73
  45.1 10.6 %collective-permute-start.10 = (f32[5,2,32,2]{3,2,1,0:T(8,128)S(1)}, f32[5,2,32,2]{3,2,1,0:T(8,128)S(1)}, u32[]{:S(2)}, u32[]{:S(2)}) collective-permute-start(f32[5,2,32,2]{3,2,1,0:T(8,128)S(1)} %get-tuple-element.39), channel_id=1, source_target_pairs={{1,0},{3,2},{5,4},{7,6},{9,8},{11,10},{13,12},{15,14},{17,16},{19,... | collective-permute-start | bytes 7688 | tf_op jit(solution)/shard_map/ppermute | solution.py:26
  55.7 0.2 slice_reduce_fusion.5
  56.1 1.5 %collective-permute-start.7 = (f32[5,2,2,128]{3,2,1,0:T(2,128)S(1)}, f32[5,2,2,128]{3,2,1,0:T(2,128)S(1)}, u32[]{:S(2)}, u32[]{:S(2)}) collective-permute-start(f32[5,2,2,128]{3,2,1,0:T(2,128)S(1)} %get-tuple-element.43), channel_id=1, source_target_pairs={{0,2},{2,4},{4,6},{6,8},{8,10},{10,12},{12,14},{14,16},{16,18},{18... | collective-permute-start | bytes 30728 | tf_op jit(solution)/shard_map/ppermute | solution.py:23
  57.5 1.3 %collective-permute-start.9 = (f32[5,2,32,2]{3,2,1,0:T(8,128)S(1)}, f32[5,2,32,2]{3,2,1,0:T(8,128)S(1)}, u32[]{:S(2)}, u32[]{:S(2)}) collective-permute-start(f32[5,2,32,2]{3,2,1,0:T(8,128)S(1)} %get-tuple-element.38), channel_id=1, source_target_pairs={{0,1},{2,3},{4,5},{6,7},{8,9},{10,11},{12,13},{14,15},{16,17},{18,... | collective-permute-start | bytes 7688 | tf_op jit(solution)/shard_map/ppermute | solution.py:23
  58.9 1.9 %collective-permute-done.9 = f32[5,2,32,2]{3,2,1,0:T(8,128)S(1)} collective-permute-done((f32[5,2,32,2]{3,2,1,0:T(8,128)S(1)}, f32[5,2,32,2]{3,2,1,0:T(8,128)S(1)}, u32[]{:S(2)}, u32[]{:S(2)}) %collective-permute-start.9) | collective-permute-done | bytes 2592 | tf_op jit(solution)/shard_map/ppermute | solution.py:23
  60.9 0.2 pad_maximum_fusion.6
  61.2 0.2 slice_multiply_fusion.13
  61.4 0.9 collective-permute-done.7
  62.7 2.3 %collective-permute-start.14 = (f32[5,2,32,2]{3,2,1,0:T(8,128)S(1)}, f32[5,2,32,2]{3,2,1,0:T(8,128)S(1)}, u32[]{:S(2)}, u32[]{:S(2)}) collective-permute-start(f32[5,2,32,2]{3,2,1,0:T(8,128)S(1)} %get-tuple-element.48), channel_id=1, source_target_pairs={{1,0},{3,2},{5,4},{7,6},{9,8},{11,10},{13,12},{15,14},{17,16},{19,... | collective-permute-start | bytes 7688 | tf_op jit(solution)/shard_map/ppermute | solution.py:26
  65.0 0.2 slice_reduce_fusion.3
  65.3 1.3 %collective-permute-start.13 = (f32[5,2,32,2]{3,2,1,0:T(8,128)S(1)}, f32[5,2,32,2]{3,2,1,0:T(8,128)S(1)}, u32[]{:S(2)}, u32[]{:S(2)}) collective-permute-start(f32[5,2,32,2]{3,2,1,0:T(8,128)S(1)} %get-tuple-element.47), channel_id=1, source_target_pairs={{0,1},{2,3},{4,5},{6,7},{8,9},{10,11},{12,13},{14,15},{16,17},{18,... | collective-permute-start | bytes 7688 | tf_op jit(solution)/shard_map/ppermute | solution.py:23
  66.6 2.6 %collective-permute-start.12 = (f32[5,2,2,128]{3,2,1,0:T(2,128)S(1)}, f32[5,2,2,128]{3,2,1,0:T(2,128)S(1)}, u32[]{:S(2)}, u32[]{:S(2)}) collective-permute-start(f32[5,2,2,128]{3,2,1,0:T(2,128)S(1)} %get-tuple-element.46), channel_id=1, source_target_pairs={{2,0},{4,2},{6,4},{8,6},{10,8},{12,10},{14,12},{16,14},{18,16},{20... | collective-permute-start | bytes 30728 | tf_op jit(solution)/shard_map/ppermute | solution.py:26
  69.4 0.2 pad_maximum_fusion.7
  69.6 0.1 maximum_divide_fusion
  69.7 0.1 slice_subtract_fusion
  69.8 0.2 divide_select_fusion
  70.1 0.3 fusion.2
  70.4 4.8 %collective-permute-done.11 = f32[5,2,2,128]{3,2,1,0:T(2,128)S(1)} collective-permute-done((f32[5,2,2,128]{3,2,1,0:T(2,128)S(1)}, f32[5,2,2,128]{3,2,1,0:T(2,128)S(1)}, u32[]{:S(2)}, u32[]{:S(2)}) %collective-permute-start.11) | collective-permute-done | bytes 10272 | tf_op jit(solution)/shard_map/ppermute | solution.py:23
  75.5 0.1 fusion.31
  75.7 7.8 %collective-permute-done.15 = f32[5,2,32,128]{3,2,1,0:T(8,128)S(1)} collective-permute-done((f32[5,2,32,128]{3,2,1,0:T(8,128)S(1)}, f32[5,2,32,128]{3,2,1,0:T(8,128)S(1)}, u32[]{:S(2)}, u32[]{:S(2)}) %collective-permute-start.15) | collective-permute-done | bytes 163872 | tf_op jit(solution)/shard_map/ppermute | solution.py:33
  83.6 9.5 %collective-permute-done.16 = f32[5,2,64,128]{3,2,1,0:T(8,128)S(1)} collective-permute-done((f32[5,2,64,128]{3,2,1,0:T(8,128)S(1)}, f32[5,2,64,128]{3,2,1,0:T(8,128)S(1)}, u32[]{:S(2)}, u32[]{:S(2)}) %collective-permute-start.16) | collective-permute-done | bytes 327712 | tf_op jit(solution)/shard_map/ppermute | solution.py:33
  93.2 9.5 %collective-permute-done.17 = f32[5,2,64,128]{3,2,1,0:T(8,128)S(1)} collective-permute-done((f32[5,2,64,128]{3,2,1,0:T(8,128)S(1)}, f32[5,2,64,128]{3,2,1,0:T(8,128)S(1)}, u32[]{:S(2)}, u32[]{:S(2)}) %collective-permute-start.17) | collective-permute-done | bytes 327712 | tf_op jit(solution)/shard_map/ppermute | solution.py:33
  103.0 0.1 fusion.70
  103.1 10.6 %collective-permute-start.21 = (f32[5,2,32,2]{3,2,1,0:T(8,128)S(1)}, f32[5,2,32,2]{3,2,1,0:T(8,128)S(1)}, u32[]{:S(2)}, u32[]{:S(2)}) collective-permute-start(f32[5,2,32,2]{3,2,1,0:T(8,128)S(1)} %get-tuple-element.32), channel_id=1, source_target_pairs={{1,0},{3,2},{5,4},{7,6},{9,8},{11,10},{13,12},{15,14},{17,16},{19,... | collective-permute-start | bytes 7688 | tf_op jit(solution)/shard_map/ppermute | solution.py:26
  113.7 0.2 slice_reduce_fusion.1
  114.0 1.5 %collective-permute-start.18 = (f32[5,2,2,128]{3,2,1,0:T(2,128)S(1)}, f32[5,2,2,128]{3,2,1,0:T(2,128)S(1)}, u32[]{:S(2)}, u32[]{:S(2)}) collective-permute-start(f32[5,2,2,128]{3,2,1,0:T(2,128)S(1)} %get-tuple-element.36), channel_id=1, source_target_pairs={{0,2},{2,4},{4,6},{6,8},{8,10},{10,12},{12,14},{14,16},{16,18},{18... | collective-permute-start | bytes 30728 | tf_op jit(solution)/shard_map/ppermute | solution.py:23
  115.5 1.3 %collective-permute-start.20 = (f32[5,2,32,2]{3,2,1,0:T(8,128)S(1)}, f32[5,2,32,2]{3,2,1,0:T(8,128)S(1)}, u32[]{:S(2)}, u32[]{:S(2)}) collective-permute-start(f32[5,2,32,2]{3,2,1,0:T(8,128)S(1)} %get-tuple-element.31), channel_id=1, source_target_pairs={{0,1},{2,3},{4,5},{6,7},{8,9},{10,11},{12,13},{14,15},{16,17},{18,... | collective-permute-start | bytes 7688 | tf_op jit(solution)/shard_map/ppermute | solution.py:23
  116.9 1.9 %collective-permute-done.20 = f32[5,2,32,2]{3,2,1,0:T(8,128)S(1)} collective-permute-done((f32[5,2,32,2]{3,2,1,0:T(8,128)S(1)}, f32[5,2,32,2]{3,2,1,0:T(8,128)S(1)}, u32[]{:S(2)}, u32[]{:S(2)}) %collective-permute-start.20) | collective-permute-done | bytes 2592 | tf_op jit(solution)/shard_map/ppermute | solution.py:23
  118.9 0.2 pad_maximum_fusion.9
  119.1 0.2 slice_multiply_fusion.12
  119.5 0.9 collective-permute-done.18
  120.5 0.7 fusion.25
  (97 shorter events, 3.4 us)
Async XLA Ops:
  0.0 4.4 %copy-start = (f32[5,2,32,128]{3,2,1,0:T(8,128)S(1)}, f32[5,2,32,128]{3,2,1,0:T(8,128)}, u32[]{:S(2)}) copy-start(f32[5,2,32,128]{3,2,1,0:T(8,128)} %param.2) | copy-start | bytes 491524
  1.2 10.2 %collective-permute-start.3 = (f32[5,2,32,2]{3,2,1,0:T(8,128)S(1)}, f32[5,2,32,2]{3,2,1,0:T(8,128)S(1)}, u32[]{:S(2)}, u32[]{:S(2)}) collective-permute-start(f32[5,2,32,2]{3,2,1,0:T(8,128)S(1)} %get-tuple-element.52), channel_id=1, source_target_pairs={{1,0},{3,2},{5,4},{7,6},{9,8},{11,10},{13,12},{15,14},{17,16},{19,... | collective-permute-start | bytes 7688 | tf_op jit(solution)/shard_map/ppermute | solution.py:26
  3.1 8.4 %collective-permute-start.2 = (f32[5,2,32,2]{3,2,1,0:T(8,128)S(1)}, f32[5,2,32,2]{3,2,1,0:T(8,128)S(1)}, u32[]{:S(2)}, u32[]{:S(2)}) collective-permute-start(f32[5,2,32,2]{3,2,1,0:T(8,128)S(1)} %get-tuple-element.51), channel_id=1, source_target_pairs={{0,1},{2,3},{4,5},{6,7},{8,9},{10,11},{12,13},{14,15},{16,17},{18,... | collective-permute-start | bytes 7688 | tf_op jit(solution)/shard_map/ppermute | solution.py:23
  4.4 8.3 %collective-permute-start.1 = (f32[5,2,2,128]{3,2,1,0:T(2,128)S(1)}, f32[5,2,2,128]{3,2,1,0:T(2,128)S(1)}, u32[]{:S(2)}, u32[]{:S(2)}) collective-permute-start(f32[5,2,2,128]{3,2,1,0:T(2,128)S(1)} %get-tuple-element.50), channel_id=1, source_target_pairs={{2,0},{4,2},{6,4},{8,6},{10,8},{12,10},{14,12},{16,14},{18,16},{20... | collective-permute-start | bytes 30728 | tf_op jit(solution)/shard_map/ppermute | solution.py:26
  11.2 6.1 %collective-permute-start = (f32[5,2,2,128]{3,2,1,0:T(2,128)S(1)}, f32[5,2,2,128]{3,2,1,0:T(2,128)S(1)}, u32[]{:S(2)}, u32[]{:S(2)}) collective-permute-start(f32[5,2,2,128]{3,2,1,0:T(2,128)S(1)} %get-tuple-element.49), channel_id=1, source_target_pairs={{0,2},{2,4},{4,6},{6,8},{8,10},{10,12},{12,14},{14,16},{16,18},{18... | collective-permute-start | bytes 30728 | tf_op jit(solution)/shard_map/ppermute | solution.py:23
  17.7 7.9 %copy-start.1 = (s32[128]{0:T(128)S(1)}, s32[128]{0:T(128)}, u32[]{:S(2)}) copy-start(s32[128]{0:T(128)} %param.3) | copy-start | bytes 1540
  17.7 7.8 %collective-permute-start.4 = (f32[5,2,32,128]{3,2,1,0:T(8,128)S(1)}, f32[5,2,32,128]{3,2,1,0:T(8,128)S(1)}, u32[]{:S(2)}, u32[]{:S(2)}) collective-permute-start(f32[5,2,32,128]{3,2,1,0:T(8,128)S(1)} %fusion.35), channel_id=1, source_target_pairs={{0,2},{2,4},{4,6},{6,8},{8,10},{10,12},{12,14},{14,16},{16,18},{18... | collective-permute-start | bytes 491528 | tf_op jit(solution)/shard_map/ppermute | solution.py:33
  25.6 9.6 %collective-permute-start.5 = (f32[5,2,64,128]{3,2,1,0:T(8,128)S(1)}, f32[5,2,64,128]{3,2,1,0:T(8,128)S(1)}, u32[]{:S(2)}, u32[]{:S(2)}) collective-permute-start(f32[5,2,64,128]{3,2,1,0:T(8,128)S(1)} %pad_maximum_fusion.5), channel_id=1, source_target_pairs={{0,2},{2,4},{4,6},{6,8},{8,10},{10,12},{12,14},{14,16},{16,18},{18... | collective-permute-start | bytes 983048 | tf_op jit(solution)/shard_map/ppermute | solution.py:33
  35.2 9.6 %collective-permute-start.6 = (f32[5,2,64,128]{3,2,1,0:T(8,128)S(1)}, f32[5,2,64,128]{3,2,1,0:T(8,128)S(1)}, u32[]{:S(2)}, u32[]{:S(2)}) collective-permute-start(f32[5,2,64,128]{3,2,1,0:T(8,128)S(1)} %broadcast_select_fusion.1), channel_id=1, source_target_pairs={{0,4},{2,6},{4,8},{6,10},{8,12},{10,14},{12,16},{14,18},{16,20},{1... | collective-permute-start | bytes 983048 | tf_op jit(solution)/shard_map/ppermute | solution.py:33
  45.1 13.7 %collective-permute-start.10 = (f32[5,2,32,2]{3,2,1,0:T(8,128)S(1)}, f32[5,2,32,2]{3,2,1,0:T(8,128)S(1)}, u32[]{:S(2)}, u32[]{:S(2)}) collective-permute-start(f32[5,2,32,2]{3,2,1,0:T(8,128)S(1)} %get-tuple-element.39), channel_id=1, source_target_pairs={{1,0},{3,2},{5,4},{7,6},{9,8},{11,10},{13,12},{15,14},{17,16},{19,... | collective-permute-start | bytes 7688 | tf_op jit(solution)/shard_map/ppermute | solution.py:26
  56.0 5.4 %collective-permute-start.8 = (f32[5,2,2,128]{3,2,1,0:T(2,128)S(1)}, f32[5,2,2,128]{3,2,1,0:T(2,128)S(1)}, u32[]{:S(2)}, u32[]{:S(2)}) collective-permute-start(f32[5,2,2,128]{3,2,1,0:T(2,128)S(1)} %get-tuple-element.44), channel_id=1, source_target_pairs={{2,0},{4,2},{6,4},{8,6},{10,8},{12,10},{14,12},{16,14},{18,16},{20... | collective-permute-start | bytes 30728 | tf_op jit(solution)/shard_map/ppermute | solution.py:26
  56.1 6.3 %collective-permute-start.7 = (f32[5,2,2,128]{3,2,1,0:T(2,128)S(1)}, f32[5,2,2,128]{3,2,1,0:T(2,128)S(1)}, u32[]{:S(2)}, u32[]{:S(2)}) collective-permute-start(f32[5,2,2,128]{3,2,1,0:T(2,128)S(1)} %get-tuple-element.43), channel_id=1, source_target_pairs={{0,2},{2,4},{4,6},{6,8},{8,10},{10,12},{12,14},{14,16},{16,18},{18... | collective-permute-start | bytes 30728 | tf_op jit(solution)/shard_map/ppermute | solution.py:23
  57.5 3.3 %collective-permute-start.9 = (f32[5,2,32,2]{3,2,1,0:T(8,128)S(1)}, f32[5,2,32,2]{3,2,1,0:T(8,128)S(1)}, u32[]{:S(2)}, u32[]{:S(2)}) collective-permute-start(f32[5,2,32,2]{3,2,1,0:T(8,128)S(1)} %get-tuple-element.38), channel_id=1, source_target_pairs={{0,1},{2,3},{4,5},{6,7},{8,9},{10,11},{12,13},{14,15},{16,17},{18,... | collective-permute-start | bytes 7688 | tf_op jit(solution)/shard_map/ppermute | solution.py:23
  62.7 6.4 %collective-permute-start.14 = (f32[5,2,32,2]{3,2,1,0:T(8,128)S(1)}, f32[5,2,32,2]{3,2,1,0:T(8,128)S(1)}, u32[]{:S(2)}, u32[]{:S(2)}) collective-permute-start(f32[5,2,32,2]{3,2,1,0:T(8,128)S(1)} %get-tuple-element.48), channel_id=1, source_target_pairs={{1,0},{3,2},{5,4},{7,6},{9,8},{11,10},{13,12},{15,14},{17,16},{19,... | collective-permute-start | bytes 7688 | tf_op jit(solution)/shard_map/ppermute | solution.py:26
  65.3 4.0 %collective-permute-start.13 = (f32[5,2,32,2]{3,2,1,0:T(8,128)S(1)}, f32[5,2,32,2]{3,2,1,0:T(8,128)S(1)}, u32[]{:S(2)}, u32[]{:S(2)}) collective-permute-start(f32[5,2,32,2]{3,2,1,0:T(8,128)S(1)} %get-tuple-element.47), channel_id=1, source_target_pairs={{0,1},{2,3},{4,5},{6,7},{8,9},{10,11},{12,13},{14,15},{16,17},{18,... | collective-permute-start | bytes 7688 | tf_op jit(solution)/shard_map/ppermute | solution.py:23
  66.6 3.8 %collective-permute-start.12 = (f32[5,2,2,128]{3,2,1,0:T(2,128)S(1)}, f32[5,2,2,128]{3,2,1,0:T(2,128)S(1)}, u32[]{:S(2)}, u32[]{:S(2)}) collective-permute-start(f32[5,2,2,128]{3,2,1,0:T(2,128)S(1)} %get-tuple-element.46), channel_id=1, source_target_pairs={{2,0},{4,2},{6,4},{8,6},{10,8},{12,10},{14,12},{16,14},{18,16},{20... | collective-permute-start | bytes 30728 | tf_op jit(solution)/shard_map/ppermute | solution.py:26
  69.1 6.1 %collective-permute-start.11 = (f32[5,2,2,128]{3,2,1,0:T(2,128)S(1)}, f32[5,2,2,128]{3,2,1,0:T(2,128)S(1)}, u32[]{:S(2)}, u32[]{:S(2)}) collective-permute-start(f32[5,2,2,128]{3,2,1,0:T(2,128)S(1)} %get-tuple-element.45), channel_id=1, source_target_pairs={{0,2},{2,4},{4,6},{6,8},{8,10},{10,12},{12,14},{14,16},{16,18},{18... | collective-permute-start | bytes 30728 | tf_op jit(solution)/shard_map/ppermute | solution.py:23
  75.7 7.8 %collective-permute-start.15 = (f32[5,2,32,128]{3,2,1,0:T(8,128)S(1)}, f32[5,2,32,128]{3,2,1,0:T(8,128)S(1)}, u32[]{:S(2)}, u32[]{:S(2)}) collective-permute-start(f32[5,2,32,128]{3,2,1,0:T(8,128)S(1)} %fusion.31), channel_id=1, source_target_pairs={{0,2},{2,4},{4,6},{6,8},{8,10},{10,12},{12,14},{14,16},{16,18},{18... | collective-permute-start | bytes 491528 | tf_op jit(solution)/shard_map/ppermute | solution.py:33
  83.5 9.6 %collective-permute-start.16 = (f32[5,2,64,128]{3,2,1,0:T(8,128)S(1)}, f32[5,2,64,128]{3,2,1,0:T(8,128)S(1)}, u32[]{:S(2)}, u32[]{:S(2)}) collective-permute-start(f32[5,2,64,128]{3,2,1,0:T(8,128)S(1)} %pad_maximum_fusion.8), channel_id=1, source_target_pairs={{0,2},{2,4},{4,6},{6,8},{8,10},{10,12},{12,14},{14,16},{16,18},{18... | collective-permute-start | bytes 983048 | tf_op jit(solution)/shard_map/ppermute | solution.py:33
  93.1 9.6 %collective-permute-start.17 = (f32[5,2,64,128]{3,2,1,0:T(8,128)S(1)}, f32[5,2,64,128]{3,2,1,0:T(8,128)S(1)}, u32[]{:S(2)}, u32[]{:S(2)}) collective-permute-start(f32[5,2,64,128]{3,2,1,0:T(8,128)S(1)} %broadcast_select_fusion), channel_id=1, source_target_pairs={{0,4},{2,6},{4,8},{6,10},{8,12},{10,14},{12,16},{14,18},{16,20},{1... | collective-permute-start | bytes 983048 | tf_op jit(solution)/shard_map/ppermute | solution.py:33
  103.1 13.7 %collective-permute-start.21 = (f32[5,2,32,2]{3,2,1,0:T(8,128)S(1)}, f32[5,2,32,2]{3,2,1,0:T(8,128)S(1)}, u32[]{:S(2)}, u32[]{:S(2)}) collective-permute-start(f32[5,2,32,2]{3,2,1,0:T(8,128)S(1)} %get-tuple-element.32), channel_id=1, source_target_pairs={{1,0},{3,2},{5,4},{7,6},{9,8},{11,10},{13,12},{15,14},{17,16},{19,... | collective-permute-start | bytes 7688 | tf_op jit(solution)/shard_map/ppermute | solution.py:26
  113.9 5.5 %collective-permute-start.19 = (f32[5,2,2,128]{3,2,1,0:T(2,128)S(1)}, f32[5,2,2,128]{3,2,1,0:T(2,128)S(1)}, u32[]{:S(2)}, u32[]{:S(2)}) collective-permute-start(f32[5,2,2,128]{3,2,1,0:T(2,128)S(1)} %get-tuple-element.37), channel_id=1, source_target_pairs={{2,0},{4,2},{6,4},{8,6},{10,8},{12,10},{14,12},{16,14},{18,16},{20... | collective-permute-start | bytes 30728 | tf_op jit(solution)/shard_map/ppermute | solution.py:26
  114.0 6.3 %collective-permute-start.18 = (f32[5,2,2,128]{3,2,1,0:T(2,128)S(1)}, f32[5,2,2,128]{3,2,1,0:T(2,128)S(1)}, u32[]{:S(2)}, u32[]{:S(2)}) collective-permute-start(f32[5,2,2,128]{3,2,1,0:T(2,128)S(1)} %get-tuple-element.36), channel_id=1, source_target_pairs={{0,2},{2,4},{4,6},{6,8},{8,10},{10,12},{12,14},{14,16},{16,18},{18... | collective-permute-start | bytes 30728 | tf_op jit(solution)/shard_map/ppermute | solution.py:23
  115.5 3.3 %collective-permute-start.20 = (f32[5,2,32,2]{3,2,1,0:T(8,128)S(1)}, f32[5,2,32,2]{3,2,1,0:T(8,128)S(1)}, u32[]{:S(2)}, u32[]{:S(2)}) collective-permute-start(f32[5,2,32,2]{3,2,1,0:T(8,128)S(1)} %get-tuple-element.31), channel_id=1, source_target_pairs={{0,1},{2,3},{4,5},{6,7},{8,9},{10,11},{12,13},{14,15},{16,17},{18,... | collective-permute-start | bytes 7688 | tf_op jit(solution)/shard_map/ppermute | solution.py:23
where the time goes:
time: 122 us; the launch traced here: 121 us
  waiting for transfers between devices  68.4 us (56%)
  starting transfers between devices  43.3 us (35%)
  other arithmetic  6.18 us (5%)
  local copies, waits for them, and re-layouts  2.5 us (2%)
    ppermute x6, waiting for transfers between devices, from_behind(): return lax.ppermute(x, axis, [(i, (i + by) % peers) for i in range(peers)])  53.5 us
    ppermute x8, starting transfers between devices, padded(): lax.ppermute(lax.slice_in_dim(block, 0, width, axis=dim), axis, backward)  34.9 us
    ppermute x8, waiting for transfers between devices, padded(): lax.ppermute(lax.slice_in_dim(block, block.shape[dim] - width, None, axis...  14.9 us
    ppermute x8, starting transfers between devices, padded(): lax.ppermute(lax.slice_in_dim(block, block.shape[dim] - width, None, axis...  8.05 us
  transfers between devices with their start and end apart: 22, of which 12 were waited for; matrix products, arithmetic and copies ran while one was open for 4% of the time, Pallas kernels for 0%

commit v1 on v0

v1 whole, which is shorter than its diff:
```python
import functools

import jax
import jax.numpy as jnp
from jax import lax
from jax.experimental import pallas as pl
from jax.experimental.pallas import tpu as pltpu
from jax.sharding import PartitionSpec as P

STEPS = 2
SMAX = 96
EDGE = 4
TILE = 8

GAMMA_GAS = 1.4
COURANT_RADIAL = 0.15
COURANT_AZIMUTH = 0.15
VISCOSITY_COEF = 1.0


def up(x, axis):
    return pltpu.roll(x, x.shape[axis] - 1, axis)


def down(x, axis):
    return pltpu.roll(x, 1, axis)


def face_speeds(velocity, axis, courant):
    face = (0.5 * courant) * (velocity + up(velocity, axis))
    return jnp.maximum(face, 0.0), jnp.minimum(face, 0.0)


def advect(field, speeds, axis):
    low = field - down(field, axis)
    high = up(low, axis)
    product = low * high
    positive = product > 0
    half = jnp.where(positive, product / jnp.where(positive, low + high, 1.0), 0.0)
    flux = speeds[0] * (field + half) + speeds[1] * up(field - half, axis)
    return flux - down(flux, axis)


def push(pressure, density, speed, axis, courant):
    compress = jnp.minimum(up(speed, axis) - down(speed, axis), 0.0)
    total = pressure + VISCOSITY_COEF * density * compress * compress
    work = total * speed
    scale = -0.5 * courant
    return scale * (up(total, axis) - down(total, axis)), scale * (up(work, axis) - down(work, axis))


def shifted(window, shift_left, rows, longest):
    bits = longest.bit_length()
    x = window
    for bit in reversed(range(bits)):
        stride = 1 << bit
        left = stride - 1
        if stride >= TILE:
            keep = -(-(rows + left) // TILE) * TILE
            chosen = min(keep, x.shape[0] - stride)
            mask = (jnp.broadcast_to(shift_left, (chosen, shift_left.shape[1])) & stride) != 0
            y = jnp.where(mask, x[stride : stride + chosen], x[:chosen])
            x = y if chosen == keep else jnp.concatenate([y, x[chosen:keep]], axis=0)
        else:
            mask = (jnp.broadcast_to(shift_left, x.shape) & stride) != 0
            x = jnp.where(mask, pltpu.roll(x, x.shape[0] - stride, 0), x)
    return x[:rows]


def kernel(n_az, n_rad, x, shifts, out, *scratch):
    (A, W0, W1, O0, O1, L0, R0, L1, R1, L2, R2, state_send, state_recv, gather_send, gather_recv,
     side_send, side_recv) = scratch
    fields, depth, width, lanes = x.shape
    behind = SMAX + EDGE
    whole = behind // width
    tail = behind % width
    tail_rows = -(-tail // TILE) * TILE
    base = tail_rows + whole * width
    hops = whole + (1 if tail else 0)
    me = lax.axis_index("az")
    position = lax.axis_index("rad")

    def az(by):
        return {"az": lax.rem(me + by + n_az, n_az)}

    def rad(by):
        return {"rad": position + by}

    barrier = pltpu.get_barrier_semaphore()
    MESH = pl.DeviceIdType.MESH
    for h in range(1, hops + 1):
        pl.semaphore_signal(barrier, inc=1, device_id=az(-h), device_id_type=MESH)
    pl.semaphore_signal(barrier, inc=1, device_id=az(1), device_id_type=MESH)

    has_left = position > 0
    has_right = position < n_rad - 1

    @pl.when(has_left)
    def _():
        pl.semaphore_signal(barrier, inc=1, device_id=rad(-1), device_id_type=MESH)

    @pl.when(has_right)
    def _():
        pl.semaphore_signal(barrier, inc=1, device_id=rad(1), device_id_type=MESH)

    A[:, :, TILE : TILE + width, :] = x[...]
    beside_me = (position + n_rad - 1) // n_rad + (2 * n_rad - 2 - position) // n_rad
    pl.semaphore_wait(barrier, hops + 1 + beside_me)

    def remote(src, dst, send, recv, where):
        return pltpu.make_async_remote_copy(
            src_ref=src, dst_ref=dst, send_sem=send, recv_sem=recv, device_id=where, device_id_type=MESH
        )

    def ring_copies(z):
        return [
            remote(x.at[:, z, width - TILE : width], A.at[:, z, 0:TILE],
                   state_send.at[0, z], state_recv.at[0, z], az(1)),
            remote(x.at[:, z, 0:TILE], A.at[:, z, TILE + width : 2 * TILE + width],
                   state_send.at[1, z], state_recv.at[1, z], az(-1)),
        ]

    def side_copies(phase, src, left_dst, right_dst, z):
        to_right = remote(src.at[:, z], left_dst.at[:, z], side_send.at[phase, 0, z],
                          side_recv.at[phase, 0, z], rad(1))
        to_left = remote(src.at[:, z], right_dst.at[:, z], side_send.at[phase, 1, z],
                         side_recv.at[phase, 1, z], rad(-1))
        return to_right, to_left

    def start_side(*args):
        to_right, to_left = side_copies(*args)

        @pl.when(has_right)
        def _():
            to_right.start()

        @pl.when(has_left)
        def _():
            to_left.start()

    def await_side(*args):
        to_right, to_left = side_copies(*args)

        @pl.when(has_left)
        def _():
            to_right.wait_recv()

        @pl.when(has_right)
        def _():
            to_left.wait_recv()

    def end_side(*args):
        to_right, to_left = side_copies(*args)

        @pl.when(has_right)
        def _():
            to_right.wait_send()

        @pl.when(has_left)
        def _():
            to_left.wait_send()

    windows = (W0, W1)
    rotated = (O0, O1)
    sides = ((x, L0, R0), (O0, L1, R1), (O1, L2, R2))

    def gather_copies(step, z):
        W = windows[step]
        copies = []
        for h in range(hops, 0, -1):
            if h > whole:
                src = W.at[:, z, base + width - tail_rows : base + width]
                dst = W.at[:, z, 0:tail_rows]
            else:
                src = W.at[:, z, base : base + width]
                dst = W.at[:, z, base - h * width : base - (h - 1) * width]
            copies.append(remote(src, dst, gather_send.at[step, h - 1, z], gather_recv.at[step, h - 1, z], az(h)))
        return copies

    def edges(own, left, right):
        rows = own.shape[0]
        lane = lax.broadcasted_iota(jnp.int32, (rows, lanes), 1)
        at = jnp.full((rows, lanes), position, jnp.int32)
        left = jnp.where(at == 0, jnp.broadcast_to(own[:, 0:1], own.shape), left)
        right = jnp.where(at == n_rad - 1, jnp.broadcast_to(own[:, lanes - 1 : lanes], own.shape), right)
        return jnp.where(lane < lanes // 2, right, left)

    def wide(own, beside):
        return jnp.concatenate([own, beside], axis=1)

    def hydro(step, z, strip, beside):
        rows = slice(TILE, TILE + width)
        tall = [strip(f) for f in range(fields)]
        az_speeds = face_speeds(tall[2] / tall[0], 0, COURANT_AZIMUTH)
        broad = [wide(tall[f][rows], beside(f, tall[f][rows])) for f in range(fields)]
        rad_speeds = face_speeds(broad[1] / broad[0], 1, COURANT_RADIAL)
        for f in range(fields):
            along = advect(tall[f], az_speeds, 0)[rows]
            across = advect(broad[f], rad_speeds, 1)[:, :lanes]
            windows[step][f, z, base : base + width, :] = tall[f][rows] - along - across
        for copy in gather_copies(step, z):
            copy.start()

    def viscous(z, state, extended):
        rho, mr, mp, mz, energy = state
        own = slice(None) if extended else slice(0, lanes)
        inverse = 1.0 / rho
        pressure = (GAMMA_GAS - 1.0) * (energy - 0.5 * (mr * mr + mp * mp + mz * mz) * inverse)
        az_m, az_e = push(pressure[:, own], rho[:, own], (mp * inverse)[:, own], 0, COURANT_AZIMUTH)
        rad_m, rad_e = push(pressure, rho, mr * inverse, 1, COURANT_RADIAL)
        return [
            rho[:, own],
            mr[:, own] + rad_m[:, own],
            mp[:, own] + az_m,
            mz[:, own],
            energy[:, own] + az_e + rad_e[:, own],
        ]

    count = width + 2 * EDGE

    for z in range(depth):
        for copy in ring_copies(z):
            copy.start()
        start_side(0, *sides[0], z)

    for z in range(depth):
        for copy in ring_copies(z):
            copy.wait_recv()
        await_side(0, *sides[0], z)
        hydro(0, z, lambda f: A[f, z], lambda f, own: edges(own, L0[f, z], R0[f, z]))

    for step in range(STEPS):
        O, L, R = sides[step + 1]
        for z in range(depth):
            for copy in gather_copies(step, z):
                copy.wait_recv()
            for f in range(fields):
                O[f, z] = shifted(windows[step][f, z], base - EDGE - shifts[...], count, base - EDGE - 4)
            start_side(step + 1, O, L, R, z)
        for z in range(depth):
            await_side(step + 1, O, L, R, z)
            state = [wide(O[f, z], edges(O[f, z], L[f, z], R[f, z])) for f in range(fields)]
            if step == STEPS - 1:
                new = viscous(z, state, False)
                for f in range(fields):
                    out[f, z] = new[f][EDGE : EDGE + width]
            else:
                new = viscous(z, state, True)
                A_rows = slice(TILE - EDGE, TILE - EDGE + count)
                for f in range(fields):
                    A[f, z, A_rows, :] = new[f][:, :lanes]
                hydro(
                    step + 1,
                    z,
                    lambda f: A[f, z],
                    lambda f, own: edges(own, *[new[f][EDGE : EDGE + width, lanes:]] * 2),
                )

    for z in range(depth):
        for copy in ring_copies(z):
            copy.wait_send()
        for phase in range(STEPS + 1):
            end_side(phase, *sides[phase], z)
        for step in range(STEPS):
            for copy in gather_copies(step, z):
                copy.wait_send()


def body(mesh, state, shifts):
    n_az, n_rad = mesh.shape["az"], mesh.shape["rad"]
    fields, depth, width, lanes = state.shape
    behind = SMAX + EDGE
    base = -(-(behind % width) // TILE) * TILE + behind // width * width
    hops = -(-behind // width)
    count = width + 2 * EDGE
    vmem = lambda rows: pltpu.VMEM((fields, depth, rows, lanes), jnp.float32)
    dma = pltpu.SemaphoreType.DMA
    return pl.pallas_call(
        functools.partial(kernel, n_az, n_rad),
        out_shape=jax.ShapeDtypeStruct(state.shape, state.dtype),
        in_specs=[pl.BlockSpec(memory_space=pltpu.VMEM)] * 2,
        out_specs=pl.BlockSpec(memory_space=pltpu.VMEM),
        scratch_shapes=[
            vmem(width + 2 * TILE),
            vmem(base + width),
            vmem(base + width),
            vmem(count),
            vmem(count),
            vmem(width),
            vmem(width),
            vmem(count),
            vmem(count),
            vmem(count),
            vmem(count),
            dma((2, depth)),
            dma((2, depth)),
            dma((STEPS, hops, depth)),
            dma((STEPS, hops, depth)),
            dma((STEPS + 1, 2, depth)),
            dma((STEPS + 1, 2, depth)),
        ],
        compiler_params=pltpu.CompilerParams(collective_id=0, has_side_effects=True),
    )(state, shifts.reshape(1, -1))


def solution(mesh):
    in_specs = (P(None, None, "az", "rad"), P("rad"))
    out_specs = P(None, None, "az", "rad")
    return jax.shard_map(
        functools.partial(body, mesh), mesh=mesh, in_specs=in_specs, out_specs=out_specs, check_vma=False
    )
```

time: 122 us -> 42.5 us (0.35)
  waiting for transfers between devices: 68.4 us -> 0 us
  starting transfers between devices: 43.3 us -> 0 us
  Pallas kernels: 0 us -> 40.7 us
  other arithmetic: 6.18 us -> 0 us
    ppermute x22 -> x0, waiting for transfers between devices: 68.4 us -> none  [the longest x6 53.5 us: from_behind(): return lax.ppermute(x, axis, [(i, (i + by) % peers) for i in range(peers)])]
    ppermute x22 -> x0, starting transfers between devices: 43.3 us -> none  [the longest x8 34.9 us: padded(): lax.ppermute(lax.slice_in_dim(block, 0, width, axis=dim), axis, backward)]
    pallas_call x0 -> x1, Pallas kernels: none -> 40.7 us  [body(): pl.pallas_call(functools.partial(kernel, n_az, n_rad), out_shape=jax.Shap...]
    slice x14 -> x0, local copies, waits for them, and re-layouts: 2.48 us -> none  [the longest x8 1.52 us: padded(): lax.slice_in_dim(block, block.shape[dim] - width, None, axis=dim)]
    select_n x26 -> x0, other arithmetic: 1.77 us -> none  [the longest x4 0.47 us: van_leer(): return jnp.where(positive, 2.0 * product / safe_sum, 0.0)]
    add x8 -> x0, other arithmetic: 1.73 us -> none  [the longest x4 0.75 us: transport(): jnp.maximum(face_speed, 0.0) * left_state]
    unnamed x4 -> x1, local copies, waits for them, and re-layouts: 0.01 us -> 1.59 us
  transfers between devices with their start and end apart: 22 -> 0, of which waited for: 12 -> 0; matrix products, arithmetic and copies ran while one was open for 4% -> 0% of each run, Pallas kernels for 0% -> 0%
where the time goes in v1:
time: 42.5 us; the launch traced here: 42.3 us
  Pallas kernels  40.7 us (96%)
  local copies, waits for them, and re-layouts  1.59 us (4%)
    pallas_call x1, Pallas kernels, body(): pl.pallas_call(functools.partial(kernel, n_az, n_rad), out_shape=jax.Shap...  40.7 us
    unnamed x1, local copies, waits for them, and re-layouts  1.59 us

profile of v1, /device:TPU:1, one launch (start us, length us, event | category | flops | bytes accessed | tf_op | source)
XLA Modules:
  0.0 42.3 jit_solution(5871211042002442744)
XLA Ops:
  0.0 40.7 %shard_map.28 = f32[5,2,32,128]{3,2,1,0:T(8,128)} custom-call(f32[5,2,32,128]{3,2,1,0:T(8,128)} %x.1, s32[1,128]{1,0:T(1,128)} %bitcast.1), custom_call_target="tpu_custom_call" | custom-call | tf_op jit(solution)/shard_map/pallas_call | solution.py:278
  40.7 1.6 %copy.4 = f32[5,2,32,128]{3,2,1,0:T(8,128)} copy(f32[5,2,32,128]{3,2,1,0:T(8,128)} %shard_map.28) | data formatting | bytes 327680

commit v2 on v1

--- a/solution.py
+++ b/solution.py
@@ -8,6 +8,7 @@
 from jax.sharding import PartitionSpec as P
 
 STEPS = 2
+SMIN = 4
 SMAX = 96
 EDGE = 4
 TILE = 8
@@ -75,22 +76,28 @@
     whole = behind // width
     tail = behind % width
     tail_rows = -(-tail // TILE) * TILE
-    base = tail_rows + whole * width
-    hops = whole + (1 if tail else 0)
+    group = whole + 1
+    base = group * width
+    first_row = width - tail_rows
     me = lax.axis_index("az")
+    place = lax.rem(me, group)
     position = lax.axis_index("rad")
 
     def az(by):
         return {"az": lax.rem(me + by + n_az, n_az)}
 
+    def member(by):
+        return {"az": me - place + lax.rem(place + by, group)}
+
     def rad(by):
         return {"rad": position + by}
 
     barrier = pltpu.get_barrier_semaphore()
     MESH = pl.DeviceIdType.MESH
-    for h in range(1, hops + 1):
-        pl.semaphore_signal(barrier, inc=1, device_id=az(-h), device_id_type=MESH)
-    pl.semaphore_signal(barrier, inc=1, device_id=az(1), device_id_type=MESH)
+    for by in (1, -1, -group):
+        pl.semaphore_signal(barrier, inc=1, device_id=az(by), device_id_type=MESH)
+    for h in range(1, group):
+        pl.semaphore_signal(barrier, inc=1, device_id=member(h), device_id_type=MESH)
 
     has_left = position > 0
     has_right = position < n_rad - 1
@@ -105,7 +112,7 @@
 
     A[:, :, TILE : TILE + width, :] = x[...]
     beside_me = (position + n_rad - 1) // n_rad + (2 * n_rad - 2 - position) // n_rad
-    pl.semaphore_wait(barrier, hops + 1 + beside_me)
+    pl.semaphore_wait(barrier, group + 2 + beside_me)
 
     def remote(src, dst, send, recv, where):
         return pltpu.make_async_remote_copy(
@@ -164,18 +171,34 @@
     rotated = (O0, O1)
     sides = ((x, L0, R0), (O0, L1, R1), (O1, L2, R2))
 
-    def gather_copies(step, z):
+    def gather_copies(step, f, z):
         W = windows[step]
-        copies = []
-        for h in range(hops, 0, -1):
-            if h > whole:
-                src = W.at[:, z, base + width - tail_rows : base + width]
-                dst = W.at[:, z, 0:tail_rows]
-            else:
-                src = W.at[:, z, base : base + width]
-                dst = W.at[:, z, base - h * width : base - (h - 1) * width]
-            copies.append(remote(src, dst, gather_send.at[step, h - 1, z], gather_recv.at[step, h - 1, z], az(h)))
-        return copies
+        own, back = W.at[f, z, base : base + width], W.at[f, z, 0:width]
+        sems = lambda h: (gather_send.at[step, h, f, z], gather_recv.at[step, h, f, z])
+        onward = remote(own, back, *sems(0), az(group))
+        inside = []
+        for h in range(1, group):
+            dst = W.at[f, z, base - h * width : base - (h - 1) * width]
+            inside.append([remote(src, dst, *sems(h), member(h)) for src in (own, back)])
+        return onward, inside
+
+    def send_own(step, f, z):
+        onward, inside = gather_copies(step, f, z)
+        onward.start()
+        for h in range(1, group):
+
+            @pl.when(place + h < group)
+            def _():
+                inside[h - 1][0].start()
+
+    def pass_on(step, f, z):
+        onward, inside = gather_copies(step, f, z)
+        onward.wait_recv()
+        for h in range(1, group):
+
+            @pl.when(place + h >= group)
+            def _():
+                inside[h - 1][1].start()
 
     def edges(own, left, right):
         rows = own.shape[0]
@@ -198,8 +221,7 @@
             along = advect(tall[f], az_speeds, 0)[rows]
             across = advect(broad[f], rad_speeds, 1)[:, :lanes]
             windows[step][f, z, base : base + width, :] = tall[f][rows] - along - across
-        for copy in gather_copies(step, z):
-            copy.start()
+            send_own(step, f, z)
 
     def viscous(z, state, extended):
         rho, mr, mp, mz, energy = state
@@ -230,12 +252,16 @@
         hydro(0, z, lambda f: A[f, z], lambda f, own: edges(own, L0[f, z], R0[f, z]))
 
     for step in range(STEPS):
+        for z in range(depth):
+            for f in range(fields):
+                pass_on(step, f, z)
         O, L, R = sides[step + 1]
         for z in range(depth):
-            for copy in gather_copies(step, z):
-                copy.wait_recv()
             for f in range(fields):
-                O[f, z] = shifted(windows[step][f, z], base - EDGE - shifts[...], count, base - EDGE - 4)
+                for copies in gather_copies(step, f, z)[1]:
+                    copies[0].wait_recv()
+                start = base - first_row - EDGE
+                O[f, z] = shifted(windows[step][f, z, first_row:], start - shifts[...], count, start - SMIN)
             start_side(step + 1, O, L, R, z)
         for z in range(depth):
             await_side(step + 1, O, L, R, z)
@@ -262,16 +288,19 @@
         for phase in range(STEPS + 1):
             end_side(phase, *sides[phase], z)
         for step in range(STEPS):
-            for copy in gather_copies(step, z):
-                copy.wait_send()
+            for f in range(fields):
+                onward, inside = gather_copies(step, f, z)
+                onward.wait_send()
+                for copies in inside:
+                    copies[0].wait_send()
 
 
 def body(mesh, state, shifts):
     n_az, n_rad = mesh.shape["az"], mesh.shape["rad"]
     fields, depth, width, lanes = state.shape
     behind = SMAX + EDGE
-    base = -(-(behind % width) // TILE) * TILE + behind // width * width
-    hops = -(-behind // width)
+    group = behind // width + 1
+    window = (group + 1) * width
     count = width + 2 * EDGE
     vmem = lambda rows: pltpu.VMEM((fields, depth, rows, lanes), jnp.float32)
     dma = pltpu.SemaphoreType.DMA
@@ -282,8 +311,8 @@
         out_specs=pl.BlockSpec(memory_space=pltpu.VMEM),
         scratch_shapes=[
             vmem(width + 2 * TILE),
-            vmem(base + width),
-            vmem(base + width),
+            vmem(window),
+            vmem(window),
             vmem(count),
             vmem(count),
             vmem(width),
@@ -294,8 +323,8 @@
             vmem(count),
             dma((2, depth)),
             dma((2, depth)),
-            dma((STEPS, hops, depth)),
-            dma((STEPS, hops, depth)),
+            dma((STEPS, group, fields, depth)),
+            dma((STEPS, group, fields, depth)),
             dma((STEPS + 1, 2, depth)),
             dma((STEPS + 1, 2, depth)),
         ],

time: 42.5 us -> 38.3 us (0.901)
  Pallas kernels: 40.7 us -> 36.5 us
    pallas_call x1, Pallas kernels: 40.7 us -> 36.5 us  [body(): pl.pallas_call(functools.partial(kernel, n_az, n_rad), out_shape=jax.Shap...]
where the time goes in v2:
time: 38.3 us; the launch traced here: 38.1 us
  Pallas kernels  36.5 us (95%)
  local copies, waits for them, and re-layouts  1.59 us (4%)
    pallas_call x1, Pallas kernels, body(): pl.pallas_call(functools.partial(kernel, n_az, n_rad), out_shape=jax.Shap...  36.5 us
    unnamed x1, local copies, waits for them, and re-layouts  1.59 us

profile of v2, /device:TPU:1, one launch (start us, length us, event | category | flops | bytes accessed | tf_op | source)
XLA Modules:
  0.0 38.1 jit_solution(17050600278154196577)
XLA Ops:
  0.0 36.5 %shard_map.28 = f32[5,2,32,128]{3,2,1,0:T(8,128)} custom-call(f32[5,2,32,128]{3,2,1,0:T(8,128)} %x.1, s32[1,128]{1,0:T(1,128)} %bitcast.1), custom_call_target="tpu_custom_call" | custom-call | tf_op jit(solution)/shard_map/pallas_call | solution.py:307
  36.5 1.6 %copy.4 = f32[5,2,32,128]{3,2,1,0:T(8,128)} copy(f32[5,2,32,128]{3,2,1,0:T(8,128)} %shard_map.28) | data formatting | bytes 327680

commit v3 on v2

--- a/solution.py
+++ b/solution.py
@@ -68,8 +68,8 @@
     return x[:rows]
 
 
-def kernel(n_az, n_rad, x, shifts, out, *scratch):
-    (A, W0, W1, O0, O1, L0, R0, L1, R1, L2, R2, state_send, state_recv, gather_send, gather_recv,
+def kernel(n_az, n_rad, x_in, shifts, out, *scratch):
+    (x, LOW, HIGH, load_sem, A, W0, W1, O0, O1, L0, R0, L1, R1, L2, R2, state_send, state_recv, relay_send, relay_recv, gather_send, gather_recv,
      side_send, side_recv) = scratch
     fields, depth, width, lanes = x.shape
     behind = SMAX + EDGE
@@ -87,14 +87,16 @@
         return {"az": lax.rem(me + by + n_az, n_az)}
 
     def member(by):
-        return {"az": me - place + lax.rem(place + by, group)}
+        return {"az": me - place + lax.rem(place + by + group, group)}
 
     def rad(by):
         return {"rad": position + by}
 
     barrier = pltpu.get_barrier_semaphore()
     MESH = pl.DeviceIdType.MESH
-    for by in (1, -1, -group):
+    load = pltpu.make_async_copy(x_in, x, load_sem)
+    load.start()
+    for by in (group, -group):
         pl.semaphore_signal(barrier, inc=1, device_id=az(by), device_id_type=MESH)
     for h in range(1, group):
         pl.semaphore_signal(barrier, inc=1, device_id=member(h), device_id_type=MESH)
@@ -110,9 +112,10 @@
     def _():
         pl.semaphore_signal(barrier, inc=1, device_id=rad(1), device_id_type=MESH)
 
+    load.wait()
     A[:, :, TILE : TILE + width, :] = x[...]
     beside_me = (position + n_rad - 1) // n_rad + (2 * n_rad - 2 - position) // n_rad
-    pl.semaphore_wait(barrier, group + 2 + beside_me)
+    pl.semaphore_wait(barrier, group + 1 + beside_me)
 
     def remote(src, dst, send, recv, where):
         return pltpu.make_async_remote_copy(
@@ -120,12 +123,44 @@
         )
 
     def ring_copies(z):
-        return [
-            remote(x.at[:, z, width - TILE : width], A.at[:, z, 0:TILE],
-                   state_send.at[0, z], state_recv.at[0, z], az(1)),
-            remote(x.at[:, z, 0:TILE], A.at[:, z, TILE + width : 2 * TILE + width],
-                   state_send.at[1, z], state_recv.at[1, z], az(-1)),
-        ]
+        pairs = []
+        for side, relayed, by, rows, dst in (
+            (0, LOW, 1, slice(width - TILE, width), slice(0, TILE)),
+            (1, HIGH, -1, slice(0, TILE), slice(TILE + width, 2 * TILE + width)),
+        ):
+            own = x.at[:, z, rows]
+            onward = remote(own, relayed.at[:, z], relay_send.at[side, z], relay_recv.at[side, z], az(by * group))
+            sems = state_send.at[side, z], state_recv.at[side, z]
+            inside = [remote(src, A.at[:, z, dst], *sems, member(by)) for src in (own, relayed.at[:, z])]
+            pairs.append((place == (group - 1 if by == 1 else 0), onward, inside))
+        return pairs
+
+    def start_ring(z):
+        for last, onward, inside in ring_copies(z):
+
+            @pl.when(last)
+            def _():
+                onward.start()
+
+            @pl.when(jnp.logical_not(last))
+            def _():
+                inside[0].start()
+
+    def relay_ring(z):
+        for last, onward, inside in ring_copies(z):
+
+            @pl.when(last)
+            def _():
+                onward.wait_recv()
+                inside[1].start()
+
+    def end_ring(z):
+        for last, onward, inside in ring_copies(z):
+            inside[0].wait_send()
+
+            @pl.when(last)
+            def _():
+                onward.wait_send()
 
     def side_copies(phase, src, left_dst, right_dst, z):
         to_right = remote(src.at[:, z], left_dst.at[:, z], side_send.at[phase, 0, z],
@@ -241,13 +276,15 @@
     count = width + 2 * EDGE
 
     for z in range(depth):
-        for copy in ring_copies(z):
-            copy.start()
+        start_ring(z)
+    for z in range(depth):
         start_side(0, *sides[0], z)
-
-    for z in range(depth):
-        for copy in ring_copies(z):
-            copy.wait_recv()
+    for z in range(depth):
+        relay_ring(z)
+
+    for z in range(depth):
+        for _, _, inside in ring_copies(z):
+            inside[0].wait_recv()
         await_side(0, *sides[0], z)
         hydro(0, z, lambda f: A[f, z], lambda f, own: edges(own, L0[f, z], R0[f, z]))
 
@@ -283,8 +320,7 @@
                 )
 
     for z in range(depth):
-        for copy in ring_copies(z):
-            copy.wait_send()
+        end_ring(z)
         for phase in range(STEPS + 1):
             end_side(phase, *sides[phase], z)
         for step in range(STEPS):
@@ -307,9 +343,13 @@
     return pl.pallas_call(
         functools.partial(kernel, n_az, n_rad),
         out_shape=jax.ShapeDtypeStruct(state.shape, state.dtype),
-        in_specs=[pl.BlockSpec(memory_space=pltpu.VMEM)] * 2,
+        in_specs=[pl.BlockSpec(memory_space=pl.ANY), pl.BlockSpec(memory_space=pltpu.VMEM)],
         out_specs=pl.BlockSpec(memory_space=pltpu.VMEM),
         scratch_shapes=[
+            vmem(width),
+            vmem(TILE),
+            vmem(TILE),
+            dma(()),
             vmem(width + 2 * TILE),
             vmem(window),
             vmem(window),
@@ -321,6 +361,8 @@
             vmem(count),
             vmem(count),
             vmem(count),
+            dma((2, depth)),
+            dma((2, depth)),
             dma((2, depth)),
             dma((2, depth)),
             dma((STEPS, group, fields, depth)),

time: 38.3 us -> 38.5 us (level)
  no operation moved by 1% of the time
where the time goes in v3:
time: 38.5 us; the launch traced here: 38.3 us
  Pallas kernels  36.7 us (95%)
  local copies, waits for them, and re-layouts  1.59 us (4%)
    pallas_call x1, Pallas kernels, body(): pl.pallas_call(functools.partial(kernel, n_az, n_rad), out_shape=jax.Shap...  36.7 us
    unnamed x1, local copies, waits for them, and re-layouts  1.59 us

profile of v3, /device:TPU:1, one launch (start us, length us, event | category | flops | bytes accessed | tf_op | source)
XLA Modules:
  0.0 38.3 jit_solution(9827644250889816994)
XLA Ops:
  0.0 36.7 %shard_map.28 = f32[5,2,32,128]{3,2,1,0:T(8,128)} custom-call(f32[5,2,32,128]{3,2,1,0:T(8,128)} %x_in.1, s32[1,128]{1,0:T(1,128)} %bitcast.1), custom_call_target="tpu_custom_call" | custom-call | tf_op jit(solution)/shard_map/pallas_call | solution.py:343
  36.7 1.6 %copy.4 = f32[5,2,32,128]{3,2,1,0:T(8,128)} copy(f32[5,2,32,128]{3,2,1,0:T(8,128)} %shard_map.28) | data formatting | bytes 327680

commit v4 on v3

--- a/solution.py
+++ b/solution.py
@@ -342,7 +342,7 @@
     dma = pltpu.SemaphoreType.DMA
     return pl.pallas_call(
         functools.partial(kernel, n_az, n_rad),
-        out_shape=jax.ShapeDtypeStruct(state.shape, state.dtype),
+        out_shape=pltpu.VMEM(state.shape, state.dtype),
         in_specs=[pl.BlockSpec(memory_space=pl.ANY), pl.BlockSpec(memory_space=pltpu.VMEM)],
         out_specs=pl.BlockSpec(memory_space=pltpu.VMEM),
         scratch_shapes=[

time: 38.5 us -> 36.9 us (0.958)
  local copies, waits for them, and re-layouts: 1.59 us -> 0.67 us
  Pallas kernels: 36.7 us -> 36.1 us
    unnamed x1, local copies, waits for them, and re-layouts: 1.59 us -> 0.67 us
    pallas_call x1, Pallas kernels: 36.7 us -> 36.1 us  [body(): pl.pallas_call(functools.partial(kernel, n_az, n_rad), out_shape=pltpu.VM...]
where the time goes in v4:
time: 36.9 us; the launch traced here: 36.8 us
  Pallas kernels  36.1 us (98%)
  local copies, waits for them, and re-layouts  0.67 us (2%)
    pallas_call x1, Pallas kernels, body(): pl.pallas_call(functools.partial(kernel, n_az, n_rad), out_shape=pltpu.VM...  36.1 us

profile of v4, /device:TPU:1, one launch (start us, length us, event | category | flops | bytes accessed | tf_op | source)
XLA Modules:
  0.0 36.8 jit_solution(8754917201639293238)
XLA Ops:
  0.0 36.1 %shard_map.28 = f32[5,2,32,128]{3,2,1,0:T(8,128)S(1)} custom-call(f32[5,2,32,128]{3,2,1,0:T(8,128)} %x_in.1, s32[1,128]{1,0:T(1,128)} %bitcast.1), custom_call_target="tpu_custom_call" | custom-call | tf_op jit(solution)/shard_map/pallas_call | solution.py:343
  36.1 0.7 %copy.4 = f32[5,2,32,128]{3,2,1,0:T(8,128)} copy(f32[5,2,32,128]{3,2,1,0:T(8,128)S(1)} %shard_map.28) | data formatting | bytes 327680

commit v5 on v4

--- a/solution.py
+++ b/solution.py
@@ -203,22 +203,30 @@
             to_left.wait_send()
 
     windows = (W0, W1)
+    parts = (((TILE, width - 2 * TILE), (0, TILE), (width - TILE, TILE)), ((0, width),))
     rotated = (O0, O1)
     sides = ((x, L0, R0), (O0, L1, R1), (O1, L2, R2))
 
-    def gather_copies(step, f, z):
+    def gather_copies(step, part, f, z):
         W = windows[step]
-        own, back = W.at[f, z, base : base + width], W.at[f, z, 0:width]
-        sems = lambda h: (gather_send.at[step, h, f, z], gather_recv.at[step, h, f, z])
+        first, rows = parts[step][part]
+        if step == 0 and part > 0:
+            f, slot = slice(None), 0
+        else:
+            slot = f
+        own, back = W.at[f, z, base + first : base + first + rows], W.at[f, z, first : first + rows]
+        index = lambda h: (step + part if step == 0 else STEPS + 1, h, slot, z)
+        sems = lambda h: (gather_send.at[index(h)], gather_recv.at[index(h)])
         onward = remote(own, back, *sems(0), az(group))
         inside = []
         for h in range(1, group):
-            dst = W.at[f, z, base - h * width : base - (h - 1) * width]
+            start = base - h * width + first
+            dst = W.at[f, z, start : start + rows]
             inside.append([remote(src, dst, *sems(h), member(h)) for src in (own, back)])
         return onward, inside
 
-    def send_own(step, f, z):
-        onward, inside = gather_copies(step, f, z)
+    def send_own(*which):
+        onward, inside = gather_copies(*which)
         onward.start()
         for h in range(1, group):
 
@@ -226,14 +234,18 @@
             def _():
                 inside[h - 1][0].start()
 
-    def pass_on(step, f, z):
-        onward, inside = gather_copies(step, f, z)
+    def pass_on(*which):
+        onward, inside = gather_copies(*which)
         onward.wait_recv()
         for h in range(1, group):
 
             @pl.when(place + h >= group)
             def _():
                 inside[h - 1][1].start()
+
+    def await_group(*which):
+        for copies in gather_copies(*which)[1]:
+            copies[0].wait_recv()
 
     def edges(own, left, right):
         rows = own.shape[0]
@@ -246,8 +258,9 @@
     def wide(own, beside):
         return jnp.concatenate([own, beside], axis=1)
 
-    def hydro(step, z, strip, beside):
-        rows = slice(TILE, TILE + width)
+    def hydro(step, z, strip, beside, which):
+        inner = step == 0 and which[0] == 0
+        rows = slice(0, width) if inner else slice(TILE, TILE + width)
         tall = [strip(f) for f in range(fields)]
         az_speeds = face_speeds(tall[2] / tall[0], 0, COURANT_AZIMUTH)
         broad = [wide(tall[f][rows], beside(f, tall[f][rows])) for f in range(fields)]
@@ -255,8 +268,15 @@
         for f in range(fields):
             along = advect(tall[f], az_speeds, 0)[rows]
             across = advect(broad[f], rad_speeds, 1)[:, :lanes]
-            windows[step][f, z, base : base + width, :] = tall[f][rows] - along - across
-            send_own(step, f, z)
+            new = tall[f][rows] - along - across
+            for part in which:
+                first, height = parts[step][part]
+                windows[step][f, z, base + first : base + first + height, :] = new[first : first + height]
+            if which[0] == 0:
+                send_own(step, 0, f, z)
+        if which[0] > 0:
+            for part in which:
+                send_own(step, part, 0, z)
 
     def viscous(z, state, extended):
         rho, mr, mp, mz, energy = state
@@ -279,24 +299,33 @@
         start_ring(z)
     for z in range(depth):
         start_side(0, *sides[0], z)
+    def first_hydro(z, which):
+        strip = (lambda f: x[f, z]) if which[0] == 0 else (lambda f: A[f, z])
+        hydro(0, z, strip, lambda f, own: edges(own, L0[f, z], R0[f, z]), which)
+
+    for z in range(depth):
+        await_side(0, *sides[0], z)
+        first_hydro(z, (0,))
     for z in range(depth):
         relay_ring(z)
-
     for z in range(depth):
         for _, _, inside in ring_copies(z):
             inside[0].wait_recv()
-        await_side(0, *sides[0], z)
-        hydro(0, z, lambda f: A[f, z], lambda f, own: edges(own, L0[f, z], R0[f, z]))
+        first_hydro(z, (1, 2))
 
     for step in range(STEPS):
         for z in range(depth):
             for f in range(fields):
-                pass_on(step, f, z)
+                pass_on(step, 0, f, z)
+        for z in range(depth):
+            for part in range(1, len(parts[step])):
+                pass_on(step, part, 0, z)
         O, L, R = sides[step + 1]
         for z in range(depth):
+            for part in range(1, len(parts[step])):
+                await_group(step, part, 0, z)
             for f in range(fields):
-                for copies in gather_copies(step, f, z)[1]:
-                    copies[0].wait_recv()
+                await_group(step, 0, f, z)
                 start = base - first_row - EDGE
                 O[f, z] = shifted(windows[step][f, z, first_row:], start - shifts[...], count, start - SMIN)
             start_side(step + 1, O, L, R, z)
@@ -317,6 +346,7 @@
                     z,
                     lambda f: A[f, z],
                     lambda f, own: edges(own, *[new[f][EDGE : EDGE + width, lanes:]] * 2),
+                    (0,),
                 )
 
     for z in range(depth):
@@ -324,11 +354,12 @@
         for phase in range(STEPS + 1):
             end_side(phase, *sides[phase], z)
         for step in range(STEPS):
-            for f in range(fields):
-                onward, inside = gather_copies(step, f, z)
-                onward.wait_send()
-                for copies in inside:
-                    copies[0].wait_send()
+            for part in range(len(parts[step])):
+                for f in range(fields if part == 0 else 1):
+                    onward, inside = gather_copies(step, part, f, z)
+                    onward.wait_send()
+                    for copies in inside:
+                        copies[0].wait_send()
 
 
 def body(mesh, state, shifts):
@@ -365,8 +396,8 @@
             dma((2, depth)),
             dma((2, depth)),
             dma((2, depth)),
-            dma((STEPS, group, fields, depth)),
-            dma((STEPS, group, fields, depth)),
+            dma((STEPS + 2, group, fields, depth)),
+            dma((STEPS + 2, group, fields, depth)),
             dma((STEPS + 1, 2, depth)),
             dma((STEPS + 1, 2, depth)),
         ],

time: 36.9 us -> 39.4 us (1.068)
  Pallas kernels: 36.1 us -> 38.6 us
    pallas_call x1, Pallas kernels: 36.1 us -> 38.6 us  [body(): pl.pallas_call(functools.partial(kernel, n_az, n_rad), out_shape=pltpu.VM...]
where the time goes in v5:
time: 39.4 us; the launch traced here: 39.3 us
  Pallas kernels  38.6 us (98%)
  local copies, waits for them, and re-layouts  0.67 us (2%)
    pallas_call x1, Pallas kernels, body(): pl.pallas_call(functools.partial(kernel, n_az, n_rad), out_shape=pltpu.VM...  38.6 us

profile of v5, /device:TPU:1, one launch (start us, length us, event | category | flops | bytes accessed | tf_op | source)
XLA Modules:
  0.0 39.3 jit_solution(15996490956101795016)
XLA Ops:
  0.0 38.6 %shard_map.28 = f32[5,2,32,128]{3,2,1,0:T(8,128)S(1)} custom-call(f32[5,2,32,128]{3,2,1,0:T(8,128)} %x_in.1, s32[1,128]{1,0:T(1,128)} %bitcast.1), custom_call_target="tpu_custom_call" | custom-call | tf_op jit(solution)/shard_map/pallas_call | solution.py:374
  38.6 0.7 %copy.4 = f32[5,2,32,128]{3,2,1,0:T(8,128)} copy(f32[5,2,32,128]{3,2,1,0:T(8,128)S(1)} %shard_map.28) | data formatting | bytes 327680

commit v6 on v5

--- a/solution.py
+++ b/solution.py
@@ -304,10 +304,10 @@
         hydro(0, z, strip, lambda f, own: edges(own, L0[f, z], R0[f, z]), which)
 
     for z in range(depth):
+        relay_ring(z)
+    for z in range(depth):
         await_side(0, *sides[0], z)
         first_hydro(z, (0,))
-    for z in range(depth):
-        relay_ring(z)
     for z in range(depth):
         for _, _, inside in ring_copies(z):
             inside[0].wait_recv()

time: 39.4 us -> 37.9 us (0.962)
  Pallas kernels: 38.6 us -> 37.1 us
    pallas_call x1, Pallas kernels: 38.6 us -> 37.1 us  [body(): pl.pallas_call(functools.partial(kernel, n_az, n_rad), out_shape=pltpu.VM...]
where the time goes in v6:
time: 37.9 us; the launch traced here: 37.7 us
  Pallas kernels  37.1 us (98%)
  local copies, waits for them, and re-layouts  0.67 us (2%)
    pallas_call x1, Pallas kernels, body(): pl.pallas_call(functools.partial(kernel, n_az, n_rad), out_shape=pltpu.VM...  37.1 us

profile of v6, /device:TPU:1, one launch (start us, length us, event | category | flops | bytes accessed | tf_op | source)
XLA Modules:
  0.0 37.7 jit_solution(14983293141814657494)
XLA Ops:
  0.0 37.1 %shard_map.28 = f32[5,2,32,128]{3,2,1,0:T(8,128)S(1)} custom-call(f32[5,2,32,128]{3,2,1,0:T(8,128)} %x_in.1, s32[1,128]{1,0:T(1,128)} %bitcast.1), custom_call_target="tpu_custom_call" | custom-call | tf_op jit(solution)/shard_map/pallas_call | solution.py:374
  37.1 0.7 %copy.4 = f32[5,2,32,128]{3,2,1,0:T(8,128)} copy(f32[5,2,32,128]{3,2,1,0:T(8,128)S(1)} %shard_map.28) | data formatting | bytes 327680

commit v7 on v2

--- a/solution.py
+++ b/solution.py
@@ -68,8 +68,8 @@
     return x[:rows]
 
 
-def kernel(n_az, n_rad, x, shifts, out, *scratch):
-    (A, W0, W1, O0, O1, L0, R0, L1, R1, L2, R2, state_send, state_recv, gather_send, gather_recv,
+def kernel(n_az, n_rad, x_in, shifts, out, *scratch):
+    (x, load_sem, A, W0, W1, O0, O1, L0, R0, L1, R1, L2, R2, state_send, state_recv, gather_send, gather_recv,
      side_send, side_recv) = scratch
     fields, depth, width, lanes = x.shape
     behind = SMAX + EDGE
@@ -87,13 +87,15 @@
         return {"az": lax.rem(me + by + n_az, n_az)}
 
     def member(by):
-        return {"az": me - place + lax.rem(place + by, group)}
+        return {"az": me - place + lax.rem(place + by + group, group)}
 
     def rad(by):
         return {"rad": position + by}
 
     barrier = pltpu.get_barrier_semaphore()
     MESH = pl.DeviceIdType.MESH
+    load = pltpu.make_async_copy(x_in, x, load_sem)
+    load.start()
     for by in (1, -1, -group):
         pl.semaphore_signal(barrier, inc=1, device_id=az(by), device_id_type=MESH)
     for h in range(1, group):
@@ -110,6 +112,7 @@
     def _():
         pl.semaphore_signal(barrier, inc=1, device_id=rad(1), device_id_type=MESH)
 
+    load.wait()
     A[:, :, TILE : TILE + width, :] = x[...]
     beside_me = (position + n_rad - 1) // n_rad + (2 * n_rad - 2 - position) // n_rad
     pl.semaphore_wait(barrier, group + 2 + beside_me)
@@ -243,8 +246,8 @@
     for z in range(depth):
         for copy in ring_copies(z):
             copy.start()
+    for z in range(depth):
         start_side(0, *sides[0], z)
-
     for z in range(depth):
         for copy in ring_copies(z):
             copy.wait_recv()
@@ -306,10 +309,12 @@
     dma = pltpu.SemaphoreType.DMA
     return pl.pallas_call(
         functools.partial(kernel, n_az, n_rad),
-        out_shape=jax.ShapeDtypeStruct(state.shape, state.dtype),
-        in_specs=[pl.BlockSpec(memory_space=pltpu.VMEM)] * 2,
+        out_shape=pltpu.VMEM(state.shape, state.dtype),
+        in_specs=[pl.BlockSpec(memory_space=pl.ANY), pl.BlockSpec(memory_space=pltpu.VMEM)],
         out_specs=pl.BlockSpec(memory_space=pltpu.VMEM),
         scratch_shapes=[
+            vmem(width),
+            dma(()),
             vmem(width + 2 * TILE),
             vmem(window),
             vmem(window),

time: 38.3 us -> 36.4 us (0.950)
  Pallas kernels: 36.5 us -> 35.5 us
  local copies, waits for them, and re-layouts: 1.59 us -> 0.67 us
    pallas_call x1, Pallas kernels: 36.5 us -> 35.5 us  [body(): pl.pallas_call(functools.partial(kernel, n_az, n_rad), out_shape=pltpu.VM...]
    unnamed x1, local copies, waits for them, and re-layouts: 1.59 us -> 0.67 us
where the time goes in v7:
time: 36.4 us; the launch traced here: 36.2 us
  Pallas kernels  35.5 us (98%)
  local copies, waits for them, and re-layouts  0.67 us (2%)
    pallas_call x1, Pallas kernels, body(): pl.pallas_call(functools.partial(kernel, n_az, n_rad), out_shape=pltpu.VM...  35.5 us

profile of v7, /device:TPU:1, one launch (start us, length us, event | category | flops | bytes accessed | tf_op | source)
XLA Modules:
  0.0 36.2 jit_solution(1343813166938977456)
XLA Ops:
  0.0 35.5 %shard_map.28 = f32[5,2,32,128]{3,2,1,0:T(8,128)S(1)} custom-call(f32[5,2,32,128]{3,2,1,0:T(8,128)} %x_in.1, s32[1,128]{1,0:T(1,128)} %bitcast.1), custom_call_target="tpu_custom_call" | custom-call | tf_op jit(solution)/shard_map/pallas_call | solution.py:310
  35.5 0.7 %copy.4 = f32[5,2,32,128]{3,2,1,0:T(8,128)} copy(f32[5,2,32,128]{3,2,1,0:T(8,128)S(1)} %shard_map.28) | data formatting | bytes 327680

commit v8 on v7

--- a/solution.py
+++ b/solution.py
@@ -130,11 +130,11 @@
                    state_send.at[1, z], state_recv.at[1, z], az(-1)),
         ]
 
-    def side_copies(phase, src, left_dst, right_dst, z):
-        to_right = remote(src.at[:, z], left_dst.at[:, z], side_send.at[phase, 0, z],
-                          side_recv.at[phase, 0, z], rad(1))
-        to_left = remote(src.at[:, z], right_dst.at[:, z], side_send.at[phase, 1, z],
-                         side_recv.at[phase, 1, z], rad(-1))
+    def side_copies(phase, src, left_dst, right_dst, f, z):
+        to_right = remote(src.at[f, z], left_dst.at[f, z], side_send.at[phase, 0, f, z],
+                          side_recv.at[phase, 0, f, z], rad(1))
+        to_left = remote(src.at[f, z], right_dst.at[f, z], side_send.at[phase, 1, f, z],
+                         side_recv.at[phase, 1, f, z], rad(-1))
         return to_right, to_left
 
     def start_side(*args):
@@ -247,11 +247,13 @@
         for copy in ring_copies(z):
             copy.start()
     for z in range(depth):
-        start_side(0, *sides[0], z)
+        for f in range(fields):
+            start_side(0, *sides[0], f, z)
     for z in range(depth):
         for copy in ring_copies(z):
             copy.wait_recv()
-        await_side(0, *sides[0], z)
+        for f in range(fields):
+            await_side(0, *sides[0], f, z)
         hydro(0, z, lambda f: A[f, z], lambda f, own: edges(own, L0[f, z], R0[f, z]))
 
     for step in range(STEPS):
@@ -265,9 +267,10 @@
                     copies[0].wait_recv()
                 start = base - first_row - EDGE
                 O[f, z] = shifted(windows[step][f, z, first_row:], start - shifts[...], count, start - SMIN)
-            start_side(step + 1, O, L, R, z)
+                start_side(step + 1, O, L, R, f, z)
         for z in range(depth):
-            await_side(step + 1, O, L, R, z)
+            for f in range(fields):
+                await_side(step + 1, O, L, R, f, z)
             state = [wide(O[f, z], edges(O[f, z], L[f, z], R[f, z])) for f in range(fields)]
             if step == STEPS - 1:
                 new = viscous(z, state, False)
@@ -289,7 +292,8 @@
         for copy in ring_copies(z):
             copy.wait_send()
         for phase in range(STEPS + 1):
-            end_side(phase, *sides[phase], z)
+            for f in range(fields):
+                end_side(phase, *sides[phase], f, z)
         for step in range(STEPS):
             for f in range(fields):
                 onward, inside = gather_copies(step, f, z)
@@ -330,8 +334,8 @@
             dma((2, depth)),
             dma((STEPS, group, fields, depth)),
             dma((STEPS, group, fields, depth)),
-            dma((STEPS + 1, 2, depth)),
-            dma((STEPS + 1, 2, depth)),
+            dma((STEPS + 1, 2, fields, depth)),
+            dma((STEPS + 1, 2, fields, depth)),
         ],
         compiler_params=pltpu.CompilerParams(collective_id=0, has_side_effects=True),
     )(state, shifts.reshape(1, -1))

time: 36.4 us -> 37.2 us (1.022)
  Pallas kernels: 35.5 us -> 36.3 us
    pallas_call x1, Pallas kernels: 35.5 us -> 36.3 us  [body(): pl.pallas_call(functools.partial(kernel, n_az, n_rad), out_shape=pltpu.VM...]
where the time goes in v8:
time: 37.2 us; the launch traced here: 37 us
  Pallas kernels  36.3 us (98%)
  local copies, waits for them, and re-layouts  0.67 us (2%)
    pallas_call x1, Pallas kernels, body(): pl.pallas_call(functools.partial(kernel, n_az, n_rad), out_shape=pltpu.VM...  36.3 us

profile of v8, /device:TPU:1, one launch (start us, length us, event | category | flops | bytes accessed | tf_op | source)
XLA Modules:
  0.0 37.0 jit_solution(1436832706317406906)
XLA Ops:
  0.0 36.3 %shard_map.28 = f32[5,2,32,128]{3,2,1,0:T(8,128)S(1)} custom-call(f32[5,2,32,128]{3,2,1,0:T(8,128)} %x_in.1, s32[1,128]{1,0:T(1,128)} %bitcast.1), custom_call_target="tpu_custom_call" | custom-call | tf_op jit(solution)/shard_map/pallas_call | solution.py:314
  36.3 0.7 %copy.4 = f32[5,2,32,128]{3,2,1,0:T(8,128)} copy(f32[5,2,32,128]{3,2,1,0:T(8,128)S(1)} %shard_map.28) | data formatting | bytes 327680
